TPU v7x, 512 devices: a whole 4x8x8 slice. The times are simulated.
512 devices in a mesh: tm: 32 (over y_lo, z), fsdp: 16 (over x, y_hi, core).
Axes of the slice: x: 4, y: 8 (y_hi: 2, y_lo: 4; y = y_hi * 4 + y_lo), z: 8, core: 2. Of those that a mesh axis runs over, the one named last changes fastest.
Arguments:
- queries: bfloat16 [128, 512, 12, 128], P('tm', 'fsdp'), may hold values from -5 to 5
- key_states: bfloat16 [128, 512, 12, 128], P('tm', 'fsdp'), may hold values from -5 to 5
- value_states: bfloat16 [128, 512, 12, 128], P('tm', 'fsdp'), may hold values from -6 to 6
- out_grad: bfloat16 [128, 512, 3072], P('tm', 'fsdp'), may hold values from -6 to 6
- out_proj: bfloat16 [1536, 3072], P('fsdp'), may hold values from -0.109375 to 0.109375
Outputs:
- query_grad: bfloat16 [128, 512, 12, 128], P('tm', 'fsdp')
- key_grad: bfloat16 [128, 512, 12, 128], P('tm', 'fsdp')
- value_grad: bfloat16 [128, 512, 12, 128], P('tm', 'fsdp')
All inputs are finite; a program needn't handle non-finite values.
Results may differ from a plain program's by a relative error of at most 0.03.
Values may be sent and summed in bfloat16 or wider, within the bound.
A program may use at most 64 MiB of HBM per device.

v0:
```python
import jax
import jax.numpy as jnp
from jax import lax
from jax.sharding import PartitionSpec as P


def attend_back(query_block, key_block, value_block, grad_block):
    score_scale = query_block.shape[-1] ** (-0.5)
    scores = (
        jnp.einsum("fphd,gphd->phfg", query_block, key_block, preferred_element_type=jnp.float32)
        * score_scale
    )
    peak = jnp.max(scores, axis=-1, keepdims=True)
    expo = jnp.exp(scores - peak)
    probs = expo / jnp.sum(expo, axis=-1, keepdims=True)
    probs_b = probs.astype(jnp.bfloat16)
    attn_out = jnp.einsum(
        "phfg,gphd->fphd", probs_b, value_block, preferred_element_type=jnp.float32
    )
    row_delta = jnp.einsum("fphd,fphd->phf", grad_block.astype(jnp.float32), attn_out)
    dprobs = jnp.einsum(
        "fphd,gphd->phfg", grad_block, value_block, preferred_element_type=jnp.float32
    )
    dscores = (probs * (dprobs - row_delta[..., None])).astype(jnp.bfloat16)
    query_grad = (
        jnp.einsum("phfg,gphd->fphd", dscores, key_block, preferred_element_type=jnp.float32)
        * score_scale
    ).astype(jnp.bfloat16)
    key_grad = (
        jnp.einsum("phfg,fphd->gphd", dscores, query_block, preferred_element_type=jnp.float32)
        * score_scale
    ).astype(jnp.bfloat16)
    value_grad = jnp.einsum(
        "phfg,fphd->gphd", probs_b, grad_block, preferred_element_type=jnp.float32
    ).astype(jnp.bfloat16)
    return (query_grad, key_grad, value_grad)


def send_back(grads):
    return (
        lax.all_to_all(grads[0], "tm", split_axis=0, concat_axis=1, tiled=True),
        lax.all_to_all(grads[1], "tm", split_axis=0, concat_axis=1, tiled=True),
        lax.all_to_all(grads[2], "tm", split_axis=0, concat_axis=1, tiled=True),
    )


def body(queries, key_states, value_states, out_grad, out_proj):
    frames_dev, pos_dev, heads, head_size = queries.shape
    width = out_grad.shape[-1]
    flat = out_grad.reshape(frames_dev * pos_dev, width)
    grad_flat = lax.dot_general(
        flat,
        lax.all_gather(out_proj, "fsdp", axis=0, tiled=True),
        (((1,), (1,)), ((), ())),
        preferred_element_type=jnp.float32,
    ).astype(jnp.bfloat16)
    grad_attn = grad_flat.reshape(frames_dev, pos_dev, heads, head_size)
    results = send_back(
        attend_back(
            lax.all_to_all(queries, "tm", split_axis=1, concat_axis=0, tiled=True),
            lax.all_to_all(key_states, "tm", split_axis=1, concat_axis=0, tiled=True),
            lax.all_to_all(value_states, "tm", split_axis=1, concat_axis=0, tiled=True),
            lax.all_to_all(grad_attn, "tm", split_axis=1, concat_axis=0, tiled=True),
        )
    )
    return (results[0], results[1], results[2])


def solution(mesh):
    return jax.shard_map(
        body,
        mesh=mesh,
        in_specs=(
            P("tm", "fsdp", None, None),
            P("tm", "fsdp", None, None),
            P("tm", "fsdp", None, None),
            P("tm", "fsdp", None),
            P("fsdp", None),
        ),
        out_specs=(
            P("tm", "fsdp", None, None),
            P("tm", "fsdp", None, None),
            P("tm", "fsdp", None, None),
        ),
        check_vma=False,
    )
```

profile of v0, /device:TPU:64, one launch (start us, length us, event | category | flops | bytes accessed | tf_op | source)
XLA Modules:
  0.0 255.6 jit_solution(9501734445395635205)
XLA Ops:
  7.2 0.0 copy-start
  7.2 0.0 all-gather.2.cloned.1.call-start
  7.2 0.7 all-gather.2.cloned.1.call-update
  7.9 2.0 copy.39
  9.9 13.2 %all-to-all-start = ((bf16[4,32,12,128]{3,2,0,1:T(8,128)(2,1)}), bf16[4,32,12,128]{3,2,0,1:T(8,128)(2,1)S(1)}, u32[]{:S(2)}, u32[]{:S(2)}) async-start(bf16[4,32,12,128]{3,2,0,1:T(8,128)(2,1)} %copy.39), calls=%async_computation | async-start | bytes 1048576 | tf_op jit(solution)/shard_map/all_to_all | solution.py:60
  23.1 2.0 copy.41
  25.0 22.8 %all-to-all-done = bf16[4,32,12,128]{3,2,0,1:T(8,128)(2,1)S(1)} async-done(((bf16[4,32,12,128]{3,2,0,1:T(8,128)(2,1)}), bf16[4,32,12,128]{3,2,0,1:T(8,128)(2,1)S(1)}, u32[]{:S(2)}, u32[]{:S(2)}) %all-to-all-start) | async-done | bytes 393248 | tf_op jit(solution)/shard_map/all_to_all | solution.py:60
  47.8 6.2 %all-to-all-start.1 = ((bf16[4,32,12,128]{3,2,0,1:T(8,128)(2,1)}), bf16[4,32,12,128]{3,2,0,1:T(8,128)(2,1)S(1)}, u32[]{:S(2)}, u32[]{:S(2)}) async-start(bf16[4,32,12,128]{3,2,0,1:T(8,128)(2,1)} %copy.41), calls=%async_computation.1 | async-start | bytes 1048576 | tf_op jit(solution)/shard_map/all_to_all | solution.py:61
  54.0 2.0 copy.45
  56.0 14.3 %all-to-all-done.1 = bf16[4,32,12,128]{3,2,0,1:T(8,128)(2,1)S(1)} async-done(((bf16[4,32,12,128]{3,2,0,1:T(8,128)(2,1)}), bf16[4,32,12,128]{3,2,0,1:T(8,128)(2,1)S(1)}, u32[]{:S(2)}, u32[]{:S(2)}) %all-to-all-start.1) | async-done | bytes 393248 | tf_op jit(solution)/shard_map/all_to_all | solution.py:61
  70.3 4.7 %all-to-all-start.3 = ((bf16[4,32,12,128]{3,2,0,1:T(8,128)(2,1)}), bf16[4,32,12,128]{3,2,0,1:T(8,128)(2,1)S(1)}, u32[]{:S(2)}, u32[]{:S(2)}) async-start(bf16[4,32,12,128]{3,2,0,1:T(8,128)(2,1)} %copy.45), calls=%async_computation.3 | async-start | bytes 1048576 | tf_op jit(solution)/shard_map/all_to_all | solution.py:62
  75.0 71.0 %all-gather.2.cloned.1.call-done = bf16[1536,3072]{1,0:T(8,128)(2,1)} async-done(((bf16[96,3072]{1,0:T(8,128)(2,1)}), bf16[1536,3072]{1,0:T(8,128)(2,1)}) %all-gather.2.cloned.1.call-update) | async-done | bytes 9437200 | tf_op jit(solution)/shard_map/all_gather | solution.py:53
  146.0 0.0 copy-done
  146.0 6.9 %convolution_convert_fusion = bf16[128,1536]{1,0:T(8,128)(2,1)S(1)} fusion(bf16[128,3072]{1,0:T(8,128)(2,1)S(1)} %bitcast.71, bf16[1536,3072]{1,0:T(8,128)(2,1)} %all-gather.2.cloned.1.call-done), kind=kOutput, calls=%fused_computation.1 | convolution fusion | flops 1208156160 | bytes 10616832 | tf_op jit(solution)/shard_map/dot_general | solution.py:51
  152.9 0.3 reshape.88
  153.2 1.1 copy.43
  154.2 0.0 all-to-all-done.3
  154.3 8.0 %all-to-all-start.2 = ((bf16[4,32,12,128]{3,0,2,1:T(4,128)(2,1)}), bf16[4,32,12,128]{3,0,2,1:T(4,128)(2,1)S(1)}, u32[]{:S(2)}, u32[]{:S(2)}) async-start(bf16[4,32,12,128]{3,0,2,1:T(4,128)(2,1)} %copy.43), calls=%async_computation.2 | async-start | bytes 786432 | tf_op jit(solution)/shard_map/all_to_all | solution.py:63
  162.3 0.2 copy.40
  162.4 0.2 copy.42
  162.6 0.2 copy.46
  162.8 0.5 fusion.16
  163.2 0.0 copy-start.1
  163.2 14.1 %all-to-all-done.2 = bf16[4,32,12,128]{3,0,2,1:T(4,128)(2,1)S(1)} async-done(((bf16[4,32,12,128]{3,0,2,1:T(4,128)(2,1)}), bf16[4,32,12,128]{3,0,2,1:T(4,128)(2,1)S(1)}, u32[]{:S(2)}, u32[]{:S(2)}) %all-to-all-start.2) | async-done | bytes 393248 | tf_op jit(solution)/shard_map/all_to_all | solution.py:63
  177.3 0.2 copy.44
  177.5 0.5 fusion.7
  178.0 0.0 copy-done.1
  178.0 1.5 fusion.4
  179.5 0.3 fusion.10
  179.9 1.2 copy.51
  181.1 4.7 %all-to-all-start.4 = ((bf16[128,1,12,128]{3,2,1,0:T(8,128)(2,1)}), bf16[128,1,12,128]{3,2,1,0:T(8,128)(2,1)S(1)}, u32[]{:S(2)}, u32[]{:S(2)}) async-start(bf16[128,1,12,128]{3,2,1,0:T(8,128)(2,1)} %copy.51), calls=%async_computation.4 | async-start | bytes 1048576 | tf_op jit(solution)/shard_map/all_to_all | solution.py:41
  185.8 0.4 fusion.9
  186.2 1.2 copy.54
  187.4 15.8 %all-to-all-done.4 = bf16[128,1,12,128]{3,2,1,0:T(8,128)(2,1)S(1)} async-done(((bf16[128,1,12,128]{3,2,1,0:T(8,128)(2,1)}), bf16[128,1,12,128]{3,2,1,0:T(8,128)(2,1)S(1)}, u32[]{:S(2)}, u32[]{:S(2)}) %all-to-all-start.4) | async-done | bytes 393248 | tf_op jit(solution)/shard_map/all_to_all | solution.py:41
  203.2 4.7 %all-to-all-start.5 = ((bf16[128,1,12,128]{3,2,1,0:T(8,128)(2,1)}), bf16[128,1,12,128]{3,2,1,0:T(8,128)(2,1)S(1)}, u32[]{:S(2)}, u32[]{:S(2)}) async-start(bf16[128,1,12,128]{3,2,1,0:T(8,128)(2,1)} %copy.54), calls=%async_computation.5 | async-start | bytes 1048576 | tf_op jit(solution)/shard_map/all_to_all | solution.py:42
  208.0 1.6 fusion.8
  209.5 1.2 copy.58
  210.7 14.8 %all-to-all-done.5 = bf16[128,1,12,128]{3,2,1,0:T(8,128)(2,1)S(1)} async-done(((bf16[128,1,12,128]{3,2,1,0:T(8,128)(2,1)}), bf16[128,1,12,128]{3,2,1,0:T(8,128)(2,1)S(1)}, u32[]{:S(2)}, u32[]{:S(2)}) %all-to-all-start.5) | async-done | bytes 393248 | tf_op jit(solution)/shard_map/all_to_all | solution.py:42
  225.5 4.7 %all-to-all-start.6 = ((bf16[128,1,12,128]{3,2,1,0:T(8,128)(2,1)}), bf16[128,1,12,128]{3,2,1,0:T(8,128)(2,1)S(1)}, u32[]{:S(2)}, u32[]{:S(2)}) async-start(bf16[128,1,12,128]{3,2,1,0:T(8,128)(2,1)} %copy.58), calls=%async_computation.6 | async-start | bytes 1048576 | tf_op jit(solution)/shard_map/all_to_all | solution.py:43
  230.3 0.1 copy.52
  230.4 0.8 copy.60
  231.2 0.1 copy.55
  231.3 0.8 copy.61
  232.1 15.7 %all-to-all-done.6 = bf16[128,1,12,128]{3,2,1,0:T(8,128)(2,1)S(1)} async-done(((bf16[128,1,12,128]{3,2,1,0:T(8,128)(2,1)}), bf16[128,1,12,128]{3,2,1,0:T(8,128)(2,1)S(1)}, u32[]{:S(2)}, u32[]{:S(2)}) %all-to-all-start.6) | async-done | bytes 393248 | tf_op jit(solution)/shard_map/all_to_all | solution.py:43
  247.8 0.1 copy.59
  247.9 0.8 copy.62
Async XLA Ops:
  7.2 138.8 %copy-start = (bf16[4,32,3072]{2,1,0:T(8,128)(2,1)S(1)}, bf16[4,32,3072]{2,1,0:T(8,128)(2,1)}, u32[]{:S(2)}) copy-start(bf16[4,32,3072]{2,1,0:T(8,128)(2,1)} %param.8) | copy-start | bytes 2359300
  7.2 138.8 %all-gather.2.cloned.1.call-start = ((), (), s32[]{:S(2)}) async-start(), calls=%async_computation.7 | async-start | bytes 10027008 | tf_op jit(solution)/shard_map/all_gather | solution.py:53
  9.9 37.9 %all-to-all-start = ((bf16[4,32,12,128]{3,2,0,1:T(8,128)(2,1)}), bf16[4,32,12,128]{3,2,0,1:T(8,128)(2,1)S(1)}, u32[]{:S(2)}, u32[]{:S(2)}) async-start(bf16[4,32,12,128]{3,2,0,1:T(8,128)(2,1)} %copy.39), calls=%async_computation | async-start | bytes 1048576 | tf_op jit(solution)/shard_map/all_to_all | solution.py:60
  47.8 22.5 %all-to-all-start.1 = ((bf16[4,32,12,128]{3,2,0,1:T(8,128)(2,1)}), bf16[4,32,12,128]{3,2,0,1:T(8,128)(2,1)S(1)}, u32[]{:S(2)}, u32[]{:S(2)}) async-start(bf16[4,32,12,128]{3,2,0,1:T(8,128)(2,1)} %copy.41), calls=%async_computation.1 | async-start | bytes 1048576 | tf_op jit(solution)/shard_map/all_to_all | solution.py:61
  70.3 84.0 %all-to-all-start.3 = ((bf16[4,32,12,128]{3,2,0,1:T(8,128)(2,1)}), bf16[4,32,12,128]{3,2,0,1:T(8,128)(2,1)S(1)}, u32[]{:S(2)}, u32[]{:S(2)}) async-start(bf16[4,32,12,128]{3,2,0,1:T(8,128)(2,1)} %copy.45), calls=%async_computation.3 | async-start | bytes 1048576 | tf_op jit(solution)/shard_map/all_to_all | solution.py:62
  154.3 23.1 %all-to-all-start.2 = ((bf16[4,32,12,128]{3,0,2,1:T(4,128)(2,1)}), bf16[4,32,12,128]{3,0,2,1:T(4,128)(2,1)S(1)}, u32[]{:S(2)}, u32[]{:S(2)}) async-start(bf16[4,32,12,128]{3,0,2,1:T(4,128)(2,1)} %copy.43), calls=%async_computation.2 | async-start | bytes 786432 | tf_op jit(solution)/shard_map/all_to_all | solution.py:63
  163.2 14.7 %copy-start.1 = (f32[12,128,128]{1,2,0:T(8,128)}, f32[12,128,128]{1,2,0:T(8,128)S(1)}, u32[]{:S(2)}) copy-start(f32[12,128,128]{1,2,0:T(8,128)S(1)} %get-tuple-element.10) | copy-start | bytes 2359300
  181.1 22.2 %all-to-all-start.4 = ((bf16[128,1,12,128]{3,2,1,0:T(8,128)(2,1)}), bf16[128,1,12,128]{3,2,1,0:T(8,128)(2,1)S(1)}, u32[]{:S(2)}, u32[]{:S(2)}) async-start(bf16[128,1,12,128]{3,2,1,0:T(8,128)(2,1)} %copy.51), calls=%async_computation.4 | async-start | bytes 1048576 | tf_op jit(solution)/shard_map/all_to_all | solution.py:41
  203.2 22.3 %all-to-all-start.5 = ((bf16[128,1,12,128]{3,2,1,0:T(8,128)(2,1)}), bf16[128,1,12,128]{3,2,1,0:T(8,128)(2,1)S(1)}, u32[]{:S(2)}, u32[]{:S(2)}) async-start(bf16[128,1,12,128]{3,2,1,0:T(8,128)(2,1)} %copy.54), calls=%async_computation.5 | async-start | bytes 1048576 | tf_op jit(solution)/shard_map/all_to_all | solution.py:42
  225.5 22.3 %all-to-all-start.6 = ((bf16[128,1,12,128]{3,2,1,0:T(8,128)(2,1)}), bf16[128,1,12,128]{3,2,1,0:T(8,128)(2,1)S(1)}, u32[]{:S(2)}, u32[]{:S(2)}) async-start(bf16[128,1,12,128]{3,2,1,0:T(8,128)(2,1)} %copy.58), calls=%async_computation.6 | async-start | bytes 1048576 | tf_op jit(solution)/shard_map/all_to_all | solution.py:43
Sparse Core Ops, SparseCore 0:
  11.3 134.6 all-gather.1
where the time goes:
time: 257 us; the launch traced here: 256 us
  waiting for transfers between devices  169 us (66%)
  starting transfers between devices  46.3 us (18%)
  local copies, waits for them, and re-layouts  14.3 us (6%)
  between operations  14.2 us (6%)
  matrix products  11.7 us (5%)
    all_gather x1, waiting for transfers between devices, body(): lax.all_gather(out_proj, 'fsdp', axis=0, tiled=True)  71 us
    all_to_all x1, waiting for transfers between devices, body(): lax.all_to_all(queries, 'tm', split_axis=1, concat_axis=0, tiled=True)  22.8 us
    all_to_all x1, waiting for transfers between devices, send_back(): lax.all_to_all(grads[0], 'tm', split_axis=0, concat_axis=1, tiled=True)  15.8 us
    all_to_all x1, waiting for transfers between devices, send_back(): lax.all_to_all(grads[2], 'tm', split_axis=0, concat_axis=1, tiled=True)  15.7 us
    all_to_all x1, waiting for transfers between devices, send_back(): lax.all_to_all(grads[1], 'tm', split_axis=0, concat_axis=1, tiled=True)  14.8 us
    all_to_all x1, waiting for transfers between devices, body(): lax.all_to_all(key_states, 'tm', split_axis=1, concat_axis=0, tiled=True)  14.3 us
    all_to_all x1, waiting for transfers between devices, body(): lax.all_to_all(grad_attn, 'tm', split_axis=1, concat_axis=0, tiled=True)  14.1 us
    all_to_all x1, starting transfers between devices, body(): lax.all_to_all(queries, 'tm', split_axis=1, concat_axis=0, tiled=True)  13.2 us
  transfers between devices with their start and end apart: 8, of which 7 were waited for; matrix products, arithmetic and copies ran while one was open for 8% of the time, Pallas kernels for 0%

commit v1 on v0

--- a/solution.py
+++ b/solution.py
@@ -1,7 +1,21 @@
+import functools
 import jax
 import jax.numpy as jnp
 from jax import lax
 from jax.sharding import PartitionSpec as P
+from jax.lax import all_to_all, axis_size
+
+
+def _review_patches(incoming_x, at_axis):
+    heap = []
+    for _ in range(axis_size("fsdp")):
+        heap.append(incoming_x)
+    z = jnp.stack(heap)
+    v1 = all_to_all(z, axis_name="fsdp", split_axis=0, concat_axis=0)
+    return jnp.concatenate(v1, at_axis)
+
+
+show_panels_now = functools.partial(_review_patches, at_axis=0)
 
 
 def attend_back(query_block, key_block, value_block, grad_block):
@@ -50,7 +64,7 @@
     flat = out_grad.reshape(frames_dev * pos_dev, width)
     grad_flat = lax.dot_general(
         flat,
-        lax.all_gather(out_proj, "fsdp", axis=0, tiled=True),
+        show_panels_now(out_proj),
         (((1,), (1,)), ((), ())),
         preferred_element_type=jnp.float32,
     ).astype(jnp.bfloat16)

time: 257 us -> 412 us (1.60)
  waiting for transfers between devices: 169 us -> 295 us
  blocking collectives: 0 us -> 22.1 us
  starting transfers between devices: 46.3 us -> 60.8 us
  between operations: 14.2 us -> 0.8 us
  local copies, waits for them, and re-layouts: 14.3 us -> 18.5 us
    all_to_all x1, waiting for transfers between devices: 22.8 us -> 211 us  [_review_patches(): v1 = all_to_all(z, axis_name='fsdp', split_axis=0, concat_axis=0)]
    all_gather x1 -> x0, waiting for transfers between devices: 71 us -> none  [body(): lax.all_gather(out_proj, 'fsdp', axis=0, tiled=True)]
    all_to_all x0 -> x1, blocking collectives: none -> 22.1 us  [body(): lax.all_to_all(queries, 'tm', split_axis=1, concat_axis=0, tiled=True)]
    all_to_all x1, waiting for transfers between devices: 0.01 us -> 16.2 us  [body(): lax.all_to_all(value_states, 'tm', split_axis=1, concat_axis=0, tiled=True)]
    all_to_all x1, starting transfers between devices: 6.15 us -> 21.4 us  [body(): lax.all_to_all(key_states, 'tm', split_axis=1, concat_axis=0, tiled=True)]
    all_to_all x1, starting transfers between devices: 4.74 us -> 13.2 us  [body(): lax.all_to_all(value_states, 'tm', split_axis=1, concat_axis=0, tiled=True)]
    all_to_all x1, starting transfers between devices: 13.2 us -> 7.14 us  [_review_patches(): v1 = all_to_all(z, axis_name='fsdp', split_axis=0, concat_axis=0)]
    another operation x0 -> x1, local copies, waits for them, and re-layouts: none -> 5.92 us  [_review_patches(): z = jnp.stack(heap)]
  transfers between devices with their start and end apart: 8 -> 7, of which waited for: 7 -> 7; matrix products, arithmetic and copies ran while one was open for 8% -> 4% of each run, Pallas kernels for 0% -> 0%
where the time goes in v1:
time: 412 us; the launch traced here: 411 us
  waiting for transfers between devices  295 us (72%)
  starting transfers between devices  60.8 us (15%)
  blocking collectives  22.1 us (5%)
  local copies, waits for them, and re-layouts  18.5 us (4%)
  matrix products  13.7 us (3%)
    all_to_all x1, waiting for transfers between devices, _review_patches(): v1 = all_to_all(z, axis_name='fsdp', split_axis=0, concat_axis=0)  211 us
    all_to_all x1, blocking collectives, body(): lax.all_to_all(queries, 'tm', split_axis=1, concat_axis=0, tiled=True)  22.1 us
    all_to_all x1, starting transfers between devices, body(): lax.all_to_all(key_states, 'tm', split_axis=1, concat_axis=0, tiled=True)  21.4 us
    all_to_all x1, waiting for transfers between devices, body(): lax.all_to_all(value_states, 'tm', split_axis=1, concat_axis=0, tiled=True)  16.2 us
    all_to_all x1, waiting for transfers between devices, send_back(): lax.all_to_all(grads[0], 'tm', split_axis=0, concat_axis=1, tiled=True)  15.8 us
    all_to_all x1, waiting for transfers between devices, send_back(): lax.all_to_all(grads[2], 'tm', split_axis=0, concat_axis=1, tiled=True)  15.7 us
    all_to_all x1, waiting for transfers between devices, send_back(): lax.all_to_all(grads[1], 'tm', split_axis=0, concat_axis=1, tiled=True)  14.7 us
    all_to_all x1, starting transfers between devices, body(): lax.all_to_all(value_states, 'tm', split_axis=1, concat_axis=0, tiled=True)  13.2 us
  transfers between devices with their start and end apart: 7, of which 7 were waited for; matrix products, arithmetic and copies ran while one was open for 4% of the time, Pallas kernels for 0%

profile of v1, /device:TPU:64, one launch (start us, length us, event | category | flops | bytes accessed | tf_op | source)
XLA Modules:
  0.0 410.7 jit_solution(4394333331313656781)
XLA Ops:
  0.6 0.0 copy-start
  0.6 2.0 copy.45
  2.7 13.2 %all-to-all-start.4 = ((bf16[4,32,12,128]{3,2,0,1:T(8,128)(2,1)}), bf16[4,32,12,128]{3,2,0,1:T(8,128)(2,1)S(1)}, u32[]{:S(2)}, u32[]{:S(2)}) async-start(bf16[4,32,12,128]{3,2,0,1:T(8,128)(2,1)} %copy.45), calls=%async_computation.4 | async-start | bytes 1048576 | tf_op jit(solution)/shard_map/all_to_all | solution.py:76
  15.9 1.2 copy.39
  17.0 16.2 %all-to-all-done.4 = bf16[4,32,12,128]{3,2,0,1:T(8,128)(2,1)S(1)} async-done(((bf16[4,32,12,128]{3,2,0,1:T(8,128)(2,1)}), bf16[4,32,12,128]{3,2,0,1:T(8,128)(2,1)S(1)}, u32[]{:S(2)}, u32[]{:S(2)}) %all-to-all-start.4) | async-done | bytes 393248 | tf_op jit(solution)/shard_map/all_to_all | solution.py:76
  33.2 22.1 %all_to_all.119 = bf16[4,32,12,128]{3,2,0,1:T(8,128)(2,1)S(1)} all-to-all(bf16[4,32,12,128]{3,2,0,1:T(8,128)(2,1)S(1)} %copy.39), channel_id=1, replica_groups=mesh['tm'=32,'fsdp'=16] {'tm'}, dimensions={1} | all-to-all | bytes 786432 | tf_op jit(solution)/shard_map/all_to_all | solution.py:74
  55.3 5.9 %stack.2 = bf16[16,96,3072]{2,1,0:T(8,128)(2,1)} broadcast(bf16[96,3072]{1,0:T(8,128)(2,1)} %param.9), dimensions={1,2} | broadcast | bytes 10027008 | tf_op jit(solution)/shard_map/stack | solution.py:13
  61.2 0.0 copy-start.1
  61.2 7.1 %all-to-all-start.2 = ((bf16[16,96,3072]{2,1,0:T(8,128)(2,1)}), bf16[16,96,3072]{2,1,0:T(8,128)(2,1)}, u32[]{:S(2)}, u32[]{:S(2)}) async-start(bf16[16,96,3072]{2,1,0:T(8,128)(2,1)} %stack.2), calls=%async_computation.2 | async-start | bytes 18874368 | tf_op jit(solution)/shard_map/all_to_all | solution.py:14
  68.4 0.0 copy-done.1
  68.4 1.0 copy.41
  69.4 210.7 %all-to-all-done.2 = bf16[16,96,3072]{2,1,0:T(8,128)(2,1)} async-done(((bf16[16,96,3072]{2,1,0:T(8,128)(2,1)}), bf16[16,96,3072]{2,1,0:T(8,128)(2,1)}, u32[]{:S(2)}, u32[]{:S(2)}) %all-to-all-start.2) | async-done | bytes 9437216 | tf_op jit(solution)/shard_map/all_to_all | solution.py:14
  280.1 21.4 %all-to-all-start.1 = ((bf16[4,32,12,128]{3,2,0,1:T(8,128)(2,1)}), bf16[4,32,12,128]{3,2,0,1:T(8,128)(2,1)S(1)}, u32[]{:S(2)}, u32[]{:S(2)}) async-start(bf16[4,32,12,128]{3,2,0,1:T(8,128)(2,1)} %copy.41), calls=%async_computation.1 | async-start | bytes 1048576 | tf_op jit(solution)/shard_map/all_to_all | solution.py:75
  301.5 0.0 copy-done
  301.5 6.9 %convolution_convert_fusion = bf16[128,1536]{1,0:T(8,128)(2,1)S(1)} fusion(bf16[128,3072]{1,0:T(8,128)(2,1)S(1)} %bitcast.72, bf16[1536,3072]{1,0:T(8,128)(2,1)} %bitcast.9), kind=kOutput, calls=%fused_computation.1 | convolution fusion | flops 1208156160 | bytes 10616832 | tf_op jit(solution)/shard_map/dot_general | solution.py:65
  308.4 0.3 reshape.94
  308.7 1.1 copy.43
  309.8 8.9 %all-to-all-done.1 = bf16[4,32,12,128]{3,2,0,1:T(8,128)(2,1)S(1)} async-done(((bf16[4,32,12,128]{3,2,0,1:T(8,128)(2,1)}), bf16[4,32,12,128]{3,2,0,1:T(8,128)(2,1)S(1)}, u32[]{:S(2)}, u32[]{:S(2)}) %all-to-all-start.1) | async-done | bytes 393248 | tf_op jit(solution)/shard_map/all_to_all | solution.py:75
  318.6 4.9 %all-to-all-start.3 = ((bf16[4,32,12,128]{3,0,2,1:T(4,128)(2,1)}), bf16[4,32,12,128]{3,0,2,1:T(4,128)(2,1)S(1)}, u32[]{:S(2)}, u32[]{:S(2)}) async-start(bf16[4,32,12,128]{3,0,2,1:T(4,128)(2,1)} %copy.43), calls=%async_computation.3 | async-start | bytes 786432 | tf_op jit(solution)/shard_map/all_to_all | solution.py:77
  323.5 0.2 copy.46
  323.7 0.2 copy.40
  323.8 0.2 copy.42
  324.0 1.3 fusion.16
  325.3 12.8 %all-to-all-done.3 = bf16[4,32,12,128]{3,0,2,1:T(4,128)(2,1)S(1)} async-done(((bf16[4,32,12,128]{3,0,2,1:T(4,128)(2,1)}), bf16[4,32,12,128]{3,0,2,1:T(4,128)(2,1)S(1)}, u32[]{:S(2)}, u32[]{:S(2)}) %all-to-all-start.3) | async-done | bytes 393248 | tf_op jit(solution)/shard_map/all_to_all | solution.py:77
  338.2 0.2 copy.44
  338.4 1.6 fusion.7
  340.0 1.5 fusion.4
  341.5 0.3 fusion.10
  341.8 1.2 copy.51
  343.0 4.7 %all-to-all-start.5 = ((bf16[128,1,12,128]{3,2,1,0:T(8,128)(2,1)}), bf16[128,1,12,128]{3,2,1,0:T(8,128)(2,1)S(1)}, u32[]{:S(2)}, u32[]{:S(2)}) async-start(bf16[128,1,12,128]{3,2,1,0:T(8,128)(2,1)} %copy.51), calls=%async_computation.5 | async-start | bytes 1048576 | tf_op jit(solution)/shard_map/all_to_all | solution.py:55
  347.8 0.4 fusion.9
  348.2 1.2 copy.54
  349.4 15.8 %all-to-all-done.5 = bf16[128,1,12,128]{3,2,1,0:T(8,128)(2,1)S(1)} async-done(((bf16[128,1,12,128]{3,2,1,0:T(8,128)(2,1)}), bf16[128,1,12,128]{3,2,1,0:T(8,128)(2,1)S(1)}, u32[]{:S(2)}, u32[]{:S(2)}) %all-to-all-start.5) | async-done | bytes 393248 | tf_op jit(solution)/shard_map/all_to_all | solution.py:55
  365.2 4.8 %all-to-all-start.6 = ((bf16[128,1,12,128]{3,2,1,0:T(8,128)(2,1)}), bf16[128,1,12,128]{3,2,1,0:T(8,128)(2,1)S(1)}, u32[]{:S(2)}, u32[]{:S(2)}) async-start(bf16[128,1,12,128]{3,2,1,0:T(8,128)(2,1)} %copy.54), calls=%async_computation.6 | async-start | bytes 1048576 | tf_op jit(solution)/shard_map/all_to_all | solution.py:56
  370.0 1.6 fusion.8
  371.5 1.2 copy.58
  372.7 14.7 %all-to-all-done.6 = bf16[128,1,12,128]{3,2,1,0:T(8,128)(2,1)S(1)} async-done(((bf16[128,1,12,128]{3,2,1,0:T(8,128)(2,1)}), bf16[128,1,12,128]{3,2,1,0:T(8,128)(2,1)S(1)}, u32[]{:S(2)}, u32[]{:S(2)}) %all-to-all-start.6) | async-done | bytes 393248 | tf_op jit(solution)/shard_map/all_to_all | solution.py:56
  387.5 4.7 %all-to-all-start.7 = ((bf16[128,1,12,128]{3,2,1,0:T(8,128)(2,1)}), bf16[128,1,12,128]{3,2,1,0:T(8,128)(2,1)S(1)}, u32[]{:S(2)}, u32[]{:S(2)}) async-start(bf16[128,1,12,128]{3,2,1,0:T(8,128)(2,1)} %copy.58), calls=%async_computation.7 | async-start | bytes 1048576 | tf_op jit(solution)/shard_map/all_to_all | solution.py:57
  392.2 0.1 copy.52
  392.3 0.8 copy.60
  393.2 0.1 copy.55
  393.3 0.8 copy.61
  394.1 15.7 %all-to-all-done.7 = bf16[128,1,12,128]{3,2,1,0:T(8,128)(2,1)S(1)} async-done(((bf16[128,1,12,128]{3,2,1,0:T(8,128)(2,1)}), bf16[128,1,12,128]{3,2,1,0:T(8,128)(2,1)S(1)}, u32[]{:S(2)}, u32[]{:S(2)}) %all-to-all-start.7) | async-done | bytes 393248 | tf_op jit(solution)/shard_map/all_to_all | solution.py:57
  409.8 0.1 copy.59
  409.9 0.8 copy.62
Async XLA Ops:
  0.6 300.9 %copy-start = (bf16[4,32,3072]{2,1,0:T(8,128)(2,1)S(1)}, bf16[4,32,3072]{2,1,0:T(8,128)(2,1)}, u32[]{:S(2)}) copy-start(bf16[4,32,3072]{2,1,0:T(8,128)(2,1)} %param.8) | copy-start | bytes 2359300
  2.7 30.5 %all-to-all-start.4 = ((bf16[4,32,12,128]{3,2,0,1:T(8,128)(2,1)}), bf16[4,32,12,128]{3,2,0,1:T(8,128)(2,1)S(1)}, u32[]{:S(2)}, u32[]{:S(2)}) async-start(bf16[4,32,12,128]{3,2,0,1:T(8,128)(2,1)} %copy.45), calls=%async_computation.4 | async-start | bytes 1048576 | tf_op jit(solution)/shard_map/all_to_all | solution.py:76
  61.2 7.2 %copy-start.1 = (bf16[4,32,12,128]{3,1,2,0:T(8,128)(2,1)S(1)}, bf16[4,32,12,128]{3,1,2,0:T(8,128)(2,1)}, u32[]{:S(2)}) copy-start(bf16[4,32,12,128]{3,1,2,0:T(8,128)(2,1)} %param.6) | copy-start | bytes 1179652
  61.2 218.9 %all-to-all-start.2 = ((bf16[16,96,3072]{2,1,0:T(8,128)(2,1)}), bf16[16,96,3072]{2,1,0:T(8,128)(2,1)}, u32[]{:S(2)}, u32[]{:S(2)}) async-start(bf16[16,96,3072]{2,1,0:T(8,128)(2,1)} %stack.2), calls=%async_computation.2 | async-start | bytes 18874368 | tf_op jit(solution)/shard_map/all_to_all | solution.py:14
  280.1 38.5 %all-to-all-start.1 = ((bf16[4,32,12,128]{3,2,0,1:T(8,128)(2,1)}), bf16[4,32,12,128]{3,2,0,1:T(8,128)(2,1)S(1)}, u32[]{:S(2)}, u32[]{:S(2)}) async-start(bf16[4,32,12,128]{3,2,0,1:T(8,128)(2,1)} %copy.41), calls=%async_computation.1 | async-start | bytes 1048576 | tf_op jit(solution)/shard_map/all_to_all | solution.py:75
  318.6 19.6 %all-to-all-start.3 = ((bf16[4,32,12,128]{3,0,2,1:T(4,128)(2,1)}), bf16[4,32,12,128]{3,0,2,1:T(4,128)(2,1)S(1)}, u32[]{:S(2)}, u32[]{:S(2)}) async-start(bf16[4,32,12,128]{3,0,2,1:T(4,128)(2,1)} %copy.43), calls=%async_computation.3 | async-start | bytes 786432 | tf_op jit(solution)/shard_map/all_to_all | solution.py:77
  343.0 22.2 %all-to-all-start.5 = ((bf16[128,1,12,128]{3,2,1,0:T(8,128)(2,1)}), bf16[128,1,12,128]{3,2,1,0:T(8,128)(2,1)S(1)}, u32[]{:S(2)}, u32[]{:S(2)}) async-start(bf16[128,1,12,128]{3,2,1,0:T(8,128)(2,1)} %copy.51), calls=%async_computation.5 | async-start | bytes 1048576 | tf_op jit(solution)/shard_map/all_to_all | solution.py:55
  365.2 22.3 %all-to-all-start.6 = ((bf16[128,1,12,128]{3,2,1,0:T(8,128)(2,1)}), bf16[128,1,12,128]{3,2,1,0:T(8,128)(2,1)S(1)}, u32[]{:S(2)}, u32[]{:S(2)}) async-start(bf16[128,1,12,128]{3,2,1,0:T(8,128)(2,1)} %copy.54), calls=%async_computation.6 | async-start | bytes 1048576 | tf_op jit(solution)/shard_map/all_to_all | solution.py:56
  387.5 22.3 %all-to-all-start.7 = ((bf16[128,1,12,128]{3,2,1,0:T(8,128)(2,1)}), bf16[128,1,12,128]{3,2,1,0:T(8,128)(2,1)S(1)}, u32[]{:S(2)}, u32[]{:S(2)}) async-start(bf16[128,1,12,128]{3,2,1,0:T(8,128)(2,1)} %copy.58), calls=%async_computation.7 | async-start | bytes 1048576 | tf_op jit(solution)/shard_map/all_to_all | solution.py:57
